TPU v7x, 256 devices: a whole 4x4x8 slice. The times are simulated.
256 devices in a mesh: dp: 2 (over core), ctx: 32 (over y, z), head: 4 (over x).
Axes of the slice: x: 4, y: 4, z: 8, core: 2. Of those that a mesh axis runs over, the one named last changes fastest.
Arguments:
- queries: bfloat16 [2, 8192, 1024], P('dp', 'ctx', 'head'), may hold values from -0.59765625 to 0.59765625
- key_vectors: bfloat16 [2, 8192, 1024], P('dp', 'ctx', 'head'), may hold values from -0.59765625 to 0.59765625
- value_vectors: bfloat16 [2, 8192, 1024], P('dp', 'ctx', 'head'), may hold values from -0.59765625 to 0.59765625
- out_cotangent: bfloat16 [2, 8192, 1024], P('dp', 'ctx'), may hold values from -6 to 6
- out_weight: bfloat16 [128, 8, 1024], P(None, 'head'), may hold values from -0.1875 to 0.1875
- log_decay: float32 [2, 8, 8192], P('dp', 'head', 'ctx'), may hold values from -1 to 0, as said below
- level_gates: float32 [2, 8, 8, 8192], P('dp', 'head', None, 'ctx'), may hold values from 0.25 to 2
Outputs:
- query_grad: bfloat16 [2, 8192, 1024], P('dp', 'ctx', 'head')
- key_grad: bfloat16 [2, 8192, 1024], P('dp', 'ctx', 'head')
- value_grad: bfloat16 [2, 8192, 1024], P('dp', 'ctx', 'head')
- decay_grad: float32 [2, 8, 8192], P('dp', 'head', 'ctx')
- gate_grad: float32 [2, 8, 8, 8192], P('dp', 'head', None, 'ctx')
- weight_grad: float32 [128, 8, 1024], P(('dp', 'ctx'), 'head')
Inputs may be any that keep to these rules, and one draw needn't show every extreme that they name: `log_decay`: log-decays of every position and head are nonpositive.
All inputs are finite; a program needn't handle non-finite values.
Results may differ from a plain program's by a relative error of at most 0.012.
The roundings to bfloat16 on the way count: a program that leaves them out, or rounds other values in their place, can miss the bound.
Values sent between devices are 32-bit elements; how exact they have to be, the bound alone decides.
A program may use at most 64 MiB of HBM per device.

v0:
```python
import jax
import jax.numpy as jnp
from jax import lax
from jax.sharding import PartitionSpec as P


def prefix(shard, axis, combine, identity):
    size, position = (lax.axis_size(axis), lax.axis_index(axis))
    everything = lax.all_gather(shard, axis)
    start = jnp.broadcast_to(jnp.asarray(identity, shard.dtype), shard.shape)

    def step(k, before):
        at = size - 1 - k
        reached = at > position
        new = combine(before, everything[at])
        return jnp.where(reached, new, before)

    return lax.fori_loop(0, size, step, start)


def bit_count(values, shifts):
    running = jnp.zeros_like(values)
    for shift_by in range(shifts):
        running = running + (jnp.right_shift(values, shift_by) > 0).astype(jnp.int32)
    return running


def level_table(row_count, local_bits):
    span_len = row_count // 2**local_bits
    span_ids = jnp.arange(row_count, dtype=jnp.int32) // span_len
    return bit_count(jnp.bitwise_xor(span_ids[:, None], span_ids[None, :]), local_bits)


def phase_a(key_rows, value_rows, decay_rows):
    cumulative = jnp.cumsum(decay_rows)
    to_end = jnp.exp(cumulative[-1] - cumulative)
    scaled = (to_end[:, None] * value_rows.astype(jnp.float32)).astype(jnp.bfloat16)
    state_rows = jnp.dot(key_rows.T, scaled, preferred_element_type=jnp.float32)
    return (state_rows, cumulative[-1])


def phase_b(
    query_rows, key_rows, value_rows, grad_rows, decay_rows, gate_rows, arriving, local_bits
):
    row_count = query_rows.shape[0]
    cumulative = jnp.cumsum(decay_rows)
    levels = level_table(row_count, local_bits)
    positions = jnp.arange(row_count, dtype=jnp.int32)
    causal = positions[:, None] >= positions[None, :]
    log_gap = cumulative[:, None] - cumulative[None, :]
    decay_mat = jnp.where(causal, jnp.exp(jnp.where(causal, log_gap, 0.0)), 0.0)
    picked = jnp.zeros((row_count, row_count), jnp.float32)
    for level_id in range(local_bits + 1):
        picked = picked + jnp.where(levels == level_id, gate_rows[level_id][:, None], 0.0)
    mixing = picked * decay_mat
    scores = jnp.dot(query_rows, key_rows.T, preferred_element_type=jnp.float32)
    weights = mixing * scores
    weights_low = weights.astype(jnp.bfloat16)
    state_low = arriving.astype(jnp.bfloat16)
    grad_float = grad_rows.astype(jnp.float32)
    projected = jnp.einsum("tc,mce->mte", query_rows, state_low, preferred_element_type=jnp.float32)
    lift_coef = gate_rows[local_bits + 1 :] * jnp.exp(cumulative)[None, :]
    attended = jnp.dot(weights_low, value_rows, preferred_element_type=jnp.float32)
    attended = attended + jnp.sum(lift_coef[:, :, None] * projected, 0)
    attended_low = attended.astype(jnp.bfloat16)
    grad_weights = jnp.dot(grad_rows, value_rows.T, preferred_element_type=jnp.float32)
    value_local = jnp.dot(weights_low.T, grad_rows, preferred_element_type=jnp.float32)
    score_grad = (grad_weights * mixing).astype(jnp.bfloat16)
    query_grad = jnp.dot(score_grad, key_rows, preferred_element_type=jnp.float32)
    key_local = jnp.dot(score_grad.T, query_rows, preferred_element_type=jnp.float32)
    plain_terms = grad_weights * scores * decay_mat
    pair_terms = plain_terms * picked
    gate_local = jnp.stack(
        [
            jnp.sum(jnp.where(levels == level_id, plain_terms, 0.0), 1)
            for level_id in range(local_bits + 1)
        ]
    )
    row_terms = jnp.sum(pair_terms, 1)
    col_terms = jnp.sum(pair_terms, 0)
    inner_prod = jnp.sum(projected * grad_float[None], 2)
    gate_far = jnp.exp(cumulative)[None, :] * inner_prod
    row_terms = row_terms + jnp.sum(lift_coef * inner_prod, 0)
    back_rows = jnp.einsum("te,mce->mtc", grad_rows, state_low, preferred_element_type=jnp.float32)
    query_grad = query_grad + jnp.sum(lift_coef[:, :, None] * back_rows, 0)
    lifted = (lift_coef[:, :, None] * grad_float[None]).astype(jnp.bfloat16)
    query_states = jnp.einsum("tc,mte->mce", query_rows, lifted, preferred_element_type=jnp.float32)
    gate_grad = jnp.concatenate([gate_local, gate_far], 0)
    return (
        attended_low,
        query_grad,
        key_local,
        value_local,
        gate_grad,
        row_terms,
        col_terms,
        query_states,
    )


def phase_c(
    key_rows, value_rows, decay_rows, returned, key_local, value_local, row_terms, col_terms
):
    cumulative = jnp.cumsum(decay_rows)
    to_end = jnp.exp(cumulative[-1] - cumulative)
    state_low = returned.astype(jnp.bfloat16)
    key_far = to_end[:, None] * jnp.dot(value_rows, state_low.T, preferred_element_type=jnp.float32)
    value_far = to_end[:, None] * jnp.dot(key_rows, state_low, preferred_element_type=jnp.float32)
    col_total = col_terms + jnp.sum(key_rows.astype(jnp.float32) * key_far, 1)
    return (key_local + key_far, value_local + value_far, row_terms - col_total)


def add_terms(earlier, later):
    return earlier + later


def local(queries, key_vectors, value_vectors, out_cotangent, out_weight, log_decay, level_gates):
    row_count = queries.shape[1]
    head_count = log_decay.shape[1]
    head_width = out_weight.shape[0]
    level_count = level_gates.shape[2]
    ctx_bits = lax.axis_size("ctx").bit_length() - 1
    local_bits = level_count - 1 - ctx_bits
    my_index = lax.axis_index("ctx")

    def heads_major(array):
        return array[0].reshape(row_count, head_count, head_width).transpose(1, 0, 2)

    query_rows = heads_major(queries)
    key_rows = heads_major(key_vectors)
    value_rows = heads_major(value_vectors)
    grad_rows = jnp.einsum(
        "td,chd->htc", out_cotangent[0], out_weight, preferred_element_type=jnp.float32
    ).astype(jnp.bfloat16)
    decay_rows = log_decay[0]
    gate_rows = level_gates[0]
    states, totals = lax.map(lambda packed: phase_a(*packed), (key_rows, value_rows, decay_rows))
    all_totals = lax.all_gather(totals[None], "ctx", axis=0, tiled=True)
    block_ids = jnp.arange(all_totals.shape[0], dtype=jnp.int32)
    before = jnp.cumsum(all_totals, 0) - all_totals
    my_before = lax.dynamic_index_in_dim(before, my_index, 0, keepdims=False)
    relation = bit_count(jnp.bitwise_xor(block_ids, my_index), ctx_bits)
    is_lower = block_ids < my_index
    log_gap = my_before[None, :] - before - all_totals
    scaling = jnp.where(is_lower[:, None], jnp.exp(jnp.where(is_lower[:, None], log_gap, 0.0)), 0.0)
    level_ids = jnp.arange(1, ctx_bits + 1, dtype=jnp.int32)
    chosen = ((relation[:, None] == level_ids[None, :]) & is_lower[:, None]).astype(jnp.float32)
    link_coef = chosen[:, :, None] * scaling[:, None, :]
    coef_part = link_coef
    arriving = jnp.einsum(
        "nmh,nhab->mhab",
        coef_part,
        lax.all_gather(states[None], "ctx", axis=0, tiled=True),
        precision=lax.Precision.HIGHEST,
    )
    results = lax.map(
        lambda packed: phase_b(*packed, local_bits),
        (
            query_rows,
            key_rows,
            value_rows,
            grad_rows,
            decay_rows,
            gate_rows,
            jnp.moveaxis(arriving, 1, 0),
        ),
    )
    attended, query_grad, key_local, value_local, gate_grad, row_terms, col_terms, query_states = (
        results
    )
    level_major = jnp.moveaxis(query_states, 1, 0)
    weight_grad = lax.psum_scatter(
        jnp.einsum("htc,td->chd", attended, out_cotangent[0], preferred_element_type=jnp.float32),
        ("dp", "ctx"),
        scatter_dimension=0,
        tiled=True,
    )
    coef_part = link_coef
    returned = lax.psum_scatter(
        jnp.einsum("nmh,mhab->nhab", coef_part, level_major, precision=lax.Precision.HIGHEST),
        "ctx",
        scatter_dimension=0,
        tiled=True,
    )[0]
    key_grad, value_grad, flow = lax.map(
        lambda packed: phase_c(*packed),
        (key_rows, value_rows, decay_rows, returned, key_local, value_local, row_terms, col_terms),
    )
    tail_sum = prefix(jnp.sum(flow, 1), "ctx", add_terms, jnp.zeros((head_count,), jnp.float32))
    decay_grad = jnp.flip(jnp.cumsum(jnp.flip(flow, 1), 1), 1) + tail_sum[:, None]

    def token_major(array):
        return (
            array.astype(jnp.bfloat16)
            .transpose(1, 0, 2)
            .reshape(1, row_count, head_count * head_width)
        )

    return (
        token_major(query_grad),
        token_major(key_grad),
        token_major(value_grad),
        decay_grad[None],
        gate_grad[None],
        weight_grad,
    )


def solution(mesh):
    placed = (
        P("dp", "ctx", "head"),
        P("dp", "ctx", "head"),
        P("dp", "ctx", "head"),
        P("dp", "ctx", None),
        P(None, "head", None),
        P("dp", "head", "ctx"),
        P("dp", "head", None, "ctx"),
    )
    return jax.shard_map(
        local,
        mesh=mesh,
        in_specs=placed,
        out_specs=(
            P("dp", "ctx", "head"),
            P("dp", "ctx", "head"),
            P("dp", "ctx", "head"),
            P("dp", "head", "ctx"),
            P("dp", "head", None, "ctx"),
            P(("dp", "ctx"), "head", None),
        ),
        check_vma=False,
    )
```

profile of v0, /device:TPU:14, one launch (start us, length us, event | category | flops | bytes accessed | tf_op | source)
XLA Modules:
  0.0 612.2 jit_solution(5135457445195946036)
XLA Ops:
  7.2 1.0 copy.68
  8.4 1.0 copy.69
  9.6 5.6 while.68
  9.6 0.7 constant_dynamic-slice_fusion.21
  10.3 0.3 reduce-window.57
  10.9 0.6 slice_dynamic-update-slice_fusion.2
  11.5 0.6 subtract_exponential_fusion.4
  12.1 0.2 fusion.126
  12.4 0.7 constant_dynamic-slice_fusion.21
  13.1 0.3 reduce-window.57
  13.7 0.6 slice_dynamic-update-slice_fusion.2
  14.3 0.6 subtract_exponential_fusion.4
  15.0 0.2 fusion.126
  15.2 0.6 copy-done.2
  16.0 1.3 dynamic-slice
  18.2 66.0 %all-reduce = f32[64]{0:T(128)S(1)} all-reduce(f32[64]{0:T(128)S(1)} %dynamic-update-slice), channel_id=2, replica_groups=mesh['dp'=2,'ctx'=32,'head'=4] {'ctx'}, use_global_device_ids=true, to_apply=%add | all-reduce | flops 64 | bytes 512
  84.6 1.0 copy.67
  85.7 1.4 fusion.78
  87.1 12.6 %all-gather.5.cloned.1.call-done = f32[64,128,128]{2,1,0:T(8,128)} async-done(((f32[2,128,128]{2,1,0:T(8,128)}), f32[64,128,128]{2,1,0:T(8,128)}) %all-gather.5.cloned.1.call-update) | async-done | bytes 4194320 | tf_op jit(solution)/shard_map/all_gather | solution.py:153
  99.7 6.4 %fusion.76 = bf16[2,5,128,128]{3,1,2,0:T(8,128)(2,1)S(1)} fusion(f32[32,2,128,128]{3,2,1,0:T(8,128)} %bitcast.313, f32[32,2]{0,1:T(2,128)S(1)} %copy.72, f32[32,5]{0,1:T(8,128)S(1)} %and_convert_fusion), kind=kOutput, calls=%fused_computation.133 | convolution fusion | flops 62914880 | bytes 4522880 | tf_op jit(solution)/shard_map/nmh,nhab->mhab/dot_general | solution.py:150
  106.1 0.3 copy.81
  106.4 16.8 %while.69 = (s32[]{:T(128)}, bf16[2,256,128]{2,1,0:T(8,128)(2,1)}, bf16[2,256,128]{2,1,0:T(8,128)(2,1)S(1)}, f32[2,256,128]{2,1,0:T(8,128)S(1)}, f32[2,256,128]{...) while((s32[]{:T(128)}, bf16[2,256,128]{2,1,0:T(8,128)(2,1)}, ...), condition=%wide.region_17.18_spmd, body=%wide.region_5.17_spmd.sunk | while | flops 235974400 | bytes 5859733 | solution.py:156
  106.5 0.3 reduce-window.59
  107.3 0.3 multiply_reduce_fusion.7
  107.9 1.1 fusion.141
  109.1 1.9 fusion.139
  111.2 0.3 fusion.140
  111.6 1.4 fusion.142
  113.1 1.3 fusion.143
  114.4 0.4 fusion.144
  114.8 0.3 reduce-window.59
  115.7 0.3 multiply_reduce_fusion.7
  116.3 1.1 fusion.141
  117.5 1.9 fusion.139
  119.4 0.2 fusion.146
  119.6 0.3 fusion.140
  120.0 1.4 fusion.142
  121.5 1.3 fusion.143
  122.8 0.4 fusion.144
  123.2 2.2 convolution_bitcast_fusion.6
  125.7 0.4 copy.84
  126.1 3.5 convolution_bitcast_fusion.5
  129.6 4.4 copy.85
  134.0 0.6 copy-done.5
  134.6 0.6 dynamic-slice.2
  136.0 0.7 reshape.324
  136.8 172.5 %all-reduce.5.cloned.1.call-done = f32[128,2,1024]{2,0,1:T(8,128)} async-done(((f32[128,2,1024]{2,0,1:T(8,128)}), f32[128,2,1024]{2,0,1:T(8,128)}) %all-reduce.5.cloned.1.call-update) | async-done | bytes 1048592
  309.3 0.8 constant_dynamic-slice_fusion.14
  310.1 0.6 copy.92
  310.7 220.5 %reduce-scatter.3.cloned.1.call-done = f32[1,2,128,128]{3,2,1,0:T(8,128)} async-done(((f32[32,2,128,128]{3,2,1,0:T(8,128)}), f32[1,2,128,128]{3,2,1,0:T(8,128)}) %reduce-scatter.3.cloned.1.call-update) | async-done | bytes 131088 | tf_op jit(solution)/shard_map/reduce_scatter | solution.py:179
  531.2 0.9 bitcast_convert_fusion.1
  532.1 5.3 while.70
  532.1 0.3 reduce-window.61
  532.8 0.6 slice.94
  533.3 0.6 subtract_exponential_fusion.5
  534.8 0.3 reduce-window.61
  535.4 0.6 slice.94
  536.0 0.6 subtract_exponential_fusion.5
  537.6 0.6 reduce-window.49
  539.2 62.6 %all-reduce.1 = f32[64]{0:T(128)S(1)} all-reduce(f32[64]{0:T(128)S(1)} %dynamic-update-slice.1), channel_id=4, replica_groups=mesh['dp'=2,'ctx'=32,'head'=4] {'ctx'}, use_global_device_ids=true, to_apply=%add.1 | all-reduce | flops 64 | bytes 512
  601.9 1.5 while.71
  603.5 0.8 copy.97
  604.2 0.8 copy.98
  605.0 0.6 add_bitcast_fusion.3
  (171 shorter events, 8.3 us)
Async XLA Ops:
  7.2 78.5 %copy-start = (bf16[1,256,1024]{2,1,0:T(8,128)(2,1)S(1)}, bf16[1,256,1024]{2,1,0:T(8,128)(2,1)}, u32[]{:S(2)}) copy-start(bf16[1,256,1024]{2,1,0:T(8,128)(2,1)} %param.18) | copy-start | bytes 1572868
  7.2 92.5 %all-gather.5.cloned.1.call-start = ((), (), s32[]{:S(2)}) async-start(), calls=%async_computation.2 | async-start | bytes 4325376 | tf_op jit(solution)/shard_map/all_gather | solution.py:153
  9.6 96.8 %copy-start.1 = (f32[1,2,8,256]{3,2,1,0:T(8,128)S(1)}, f32[1,2,8,256]{3,2,1,0:T(8,128)}, u32[]{:S(2)}) copy-start(f32[1,2,8,256]{3,2,1,0:T(8,128)} %param.21) | copy-start | bytes 49156
  15.2 0.7 copy-start.2
  15.2 91.2 %copy-start.3 = (f32[2,256]{1,0:T(2,128)S(1)}, f32[2,256]{1,0:T(2,128)}, u32[]{:S(2)}) copy-start(f32[2,256]{1,0:T(2,128)} %get-tuple-element.1113) | copy-start | bytes 6148
  15.9 293.4 %all-reduce.5.cloned.1.call-start = ((), (), s32[]{:S(2)}) async-start(), calls=%async_computation.3 | async-start | bytes 2097152
  107.8 1.2 copy-start.6
  111.0 3.5 copy-start.7
  116.2 1.2 copy-start.6
  119.4 3.5 copy-start.7
  123.2 6.4 %copy-start.4 = (f32[2,8,256]{2,1,0:T(8,128)}, f32[2,8,256]{2,1,0:T(8,128)S(1)}, u32[]{:S(2)}) copy-start(f32[2,8,256]{2,1,0:T(8,128)S(1)} %get-tuple-element.430) | copy-start | bytes 49156
  125.5 405.7 %reduce-scatter.3.cloned.1.call-start = ((), (), s32[]{:S(2)}) async-start(), calls=%async_computation.1 | async-start | bytes 4325376 | tf_op jit(solution)/shard_map/reduce_scatter | solution.py:179
  134.0 0.7 copy-start.5
Sparse Core Ops, SparseCore 0:
  16.0 83.5 all-gather.4
  125.6 183.6 all-reduce.4
  313.7 217.4 reduce-scatter.2
where the time goes:
time: 623 us; the launch traced here: 612 us
  waiting for transfers between devices  406 us (65%)
  blocking collectives  129 us (21%)
  matrix products  28.9 us (5%)
  local copies, waits for them, and re-layouts  23.1 us (4%)
  between operations  15.4 us (2%)
  other arithmetic  8.72 us (1%)
    reduce_scatter x1, waiting for transfers between devices, local(): lax.psum_scatter(jnp.einsum('nmh,mhab->nhab', coef_part, level_major, pre...  220 us
    unnamed x4, waiting for transfers between devices  173 us
    unnamed x2, blocking collectives  129 us
    all_gather x1, waiting for transfers between devices, local(): lax.all_gather(states[None], 'ctx', axis=0, tiled=True)  12.6 us
  transfers between devices with their start and end apart: 3, of which 3 were waited for; matrix products, arithmetic and copies ran while one was open for 3% of the time, Pallas kernels for 0%

commit v1 on v0

v1 whole, which is shorter than its diff:
```python
import jax
import jax.numpy as jnp
from jax import lax
from jax.experimental import pallas as pl
from jax.experimental.pallas import tpu as pltpu
from jax.sharding import PartitionSpec as P

F32 = jnp.float32
BF16 = jnp.bfloat16
MESH = pl.DeviceIdType.MESH
NZ = 8
NY = 4
ROWS = 256
DH = 128
SPAN = 64
FAR = 5

NN = (((1,), (0,)), ((), ()))
NT = (((1,), (1,)), ((), ()))
TN = (((0,), (0,)), ((), ()))


def dot(a, b, dims):
    return lax.dot_general(a, b, dims, preferred_element_type=F32)


def iota(shape, dim):
    return lax.broadcasted_iota(jnp.int32, shape, dim)


def exact_dot(x, ones):
    hi = x.astype(BF16)
    rest = x - hi.astype(F32)
    mid = rest.astype(BF16)
    low = (rest - mid.astype(F32)).astype(BF16)
    return dot(hi, ones, NN) + dot(mid, ones, NN) + dot(low, ones, NN)


D_ROW = 0
D_COL = D_ROW + 8
F_ROW = D_COL + 4
F_COL = F_ROW + 8
S_UP = F_COL + 4
S_DOWN = S_UP + 8
T_UP = S_DOWN + 8
T_DOWN = T_UP + 4
Q_STEP = T_DOWN + 4
R_UP = Q_STEP + 10
R_DOWN = R_UP + 8
W_DP = R_DOWN + 8
W_Y = W_DP + 1
W_Z = W_Y + 6
COPIES = W_Z + 8


def kernel(
    q_ref, k_ref, v_ref, cot_ref, ow_ref, decay_ref, gates_ref,
    qg_ref, kg_ref, vg_ref, dg_ref, gg_ref, wg_ref,
    x_ref, xt_ref, zc_ref, zt_ref, flow_ref,
    dbuf, dcol, fbuf, fcol, etab, ctab,
    sbuf, tbuf, qs_ref, qa, qb, qc, qb2, qc2, pbuf, rsend, rrecv,
    g_ref, lifted_ref, lev_ref, attl_ref, qloc, kloc, vloc, att_ref,
    wbuf, wdp, usum, wa1, wb1, wa2, wb2, sa2, sb2, zsum, wz,
    ssem, rsem,
):
    ctx = lax.axis_index("ctx")
    dp = lax.axis_index("dp")
    y = lax.div(ctx, NZ)
    z = lax.rem(ctx, NZ)

    def zz(j):
        return lax.rem(z + j + NZ, NZ)

    def yy(j):
        return lax.rem(y + j + NY, NY)

    def at_z(j):
        return {"ctx": y * NZ + zz(j)}

    def at_y(j):
        return {"ctx": yy(j) * NZ + z}

    other = {"dp": 1 - dp}
    sent = []

    def copy(src, dst, n, where):
        return pltpu.make_async_remote_copy(
            src_ref=src, dst_ref=dst, send_sem=ssem.at[n], recv_sem=rsem.at[n],
            device_id=where, device_id_type=MESH,
        )

    def send(src, dst, n, where):
        c = copy(src, dst, n, where)
        c.start()
        sent.append(c)

    def arrived(dst, n, where):
        copy(dst, dst, n, where).wait_recv()

    barrier = pltpu.get_barrier_semaphore()
    for j in range(1, NZ):
        pl.semaphore_signal(barrier, inc=1, device_id=at_z(j), device_id_type=MESH)
    for j in range(1, NY):
        pl.semaphore_signal(barrier, inc=1, device_id=at_y(j), device_id_type=MESH)
    pl.semaphore_signal(barrier, inc=1, device_id=other, device_id_type=MESH)

    x_ref[...] = jnp.zeros_like(x_ref)
    x_ref[0:16, :] = gates_ref[...]
    x_ref[16:18, :] = decay_ref[...]
    upto = (iota((ROWS, ROWS), 0) <= iota((ROWS, ROWS), 1)).astype(BF16)
    cum = exact_dot(x_ref[16:24, :], upto)
    x_ref[24:32, :] = cum
    xt_ref[...] = jnp.transpose(x_ref[...])
    total = jnp.broadcast_to(cum[:, ROWS - 1 : ROWS], (8, 128))
    dbuf[pl.ds(z, 1)] = total[None]

    def cols(h):
        return slice(h * DH, (h + 1) * DH)

    def cum_col(h):
        return xt_ref[:, 24 + h : 25 + h]

    def to_end(h):
        return jnp.exp(x_ref[24 + h : 25 + h, ROWS - 1 : ROWS] - cum_col(h))

    def lift(h, m):
        return xt_ref[:, h * 8 + 3 + m : h * 8 + 4 + m] * jnp.exp(cum_col(h))

    for h in range(2):
        scaled = (to_end(h) * v_ref[:, cols(h)].astype(F32)).astype(BF16)
        sbuf[pl.ds(z, 1), h] = dot(k_ref[:, cols(h)], scaled, TN)[None]

    pl.semaphore_wait(barrier, NZ - 1 + NY - 1 + 1)

    for j in range(1, NZ):
        send(dbuf.at[z], dbuf.at[z], D_ROW + j, at_z(j))
    for h in range(2):
        send(sbuf.at[z, h], sbuf.at[z, h], S_UP + h, at_z(1))
        send(sbuf.at[z, h], sbuf.at[z, h], S_DOWN + h, at_z(-1))

    mixed = dot(cot_ref[...], ow_ref[...], NT).astype(BF16)
    ri, ci = iota((ROWS, ROWS), 0), iota((ROWS, ROWS), 1)
    perm = (ri == 2 * (ci & (DH - 1)) + jnp.right_shift(ci, 7)).astype(BF16)
    g_ref[...] = dot(mixed, perm, NN).astype(BF16)

    def make_qs(h):
        g = g_ref[:, cols(h)].astype(F32)
        for m in range(FAR):
            lifted_ref[h, :, m * DH : (m + 1) * DH] = (lift(h, m) * g).astype(BF16)
        allq = dot(q_ref[:, cols(h)], lifted_ref[h], TN)
        for m in range(FAR):
            qs_ref[h, m] = allq[:, m * DH : (m + 1) * DH]

    for h in range(2):
        make_qs(h)
        send(qs_ref.at[h, 4], qc.at[h], Q_STEP + h, at_y(-1))
        send(qs_ref.at[h, 4], qb.at[h], Q_STEP + 2 + h, at_y(1))
        send(qs_ref.at[h, 3], qa.at[h], Q_STEP + 4 + h, at_y(-1))

    for j in range(1, NZ):
        arrived(dbuf.at[zz(-j)], D_ROW + j, at_z(j))
    zero = jnp.zeros((8, 128), F32)
    running = zero
    before = []
    mine = zero
    for i in range(NZ):
        before.append(running)
        d = dbuf[i]
        mine = mine + jnp.where(i < z, d, zero)
        running = running + d
    row_total = running
    for i in range(NZ):
        after = before[i] + dbuf[i]
        etab[i] = jnp.exp(row_total - after)
        low = i < z
        ctab[i] = jnp.where(low, jnp.exp(jnp.where(low, mine - after, zero)), zero)
    dcol[pl.ds(y, 1), 0:8, :] = row_total[None]
    dcol[pl.ds(y, 1), 8:16, :] = mine[None]
    for j in range(1, NY):
        send(dcol.at[y], dcol.at[y], D_COL + j, at_y(j))

    def gather_step(k):
        for h in range(2):
            if k < 3 or h == 0:
                arrived(sbuf.at[zz(-k), h], S_UP + 2 * (k - 1) + h, at_z(1))
                send(sbuf.at[zz(-k), h], sbuf.at[zz(-k), h], S_UP + 2 * k + h, at_z(1))
            if k < 3 or h == 1:
                arrived(sbuf.at[zz(k), h], S_DOWN + 2 * (k - 1) + h, at_z(-1))
                send(sbuf.at[zz(k), h], sbuf.at[zz(k), h], S_DOWN + 2 * k + h, at_z(-1))

    def attend(h):
        q, k, v, g = q_ref[:, cols(h)], k_ref[:, cols(h)], v_ref[:, cols(h)], g_ref[:, cols(h)]
        rows, columns = iota((ROWS, ROWS), 0), iota((ROWS, ROWS), 1)
        causal = rows >= columns
        split = jnp.bitwise_xor(jnp.right_shift(rows, 6), jnp.right_shift(columns, 6))
        gap = cum_col(h) - x_ref[24 + h : 25 + h, :]
        decay = jnp.where(causal, jnp.exp(jnp.where(causal, gap, 0.0)), 0.0)
        gate = [xt_ref[:, h * 8 + l : h * 8 + l + 1] for l in range(3)]
        picked = jnp.where(split == 0, gate[0], jnp.where(split == 1, gate[1], gate[2]))
        mixing = picked * decay
        scores = dot(q, k, NT)
        gw = dot(g, v, NT)
        weights = (mixing * scores).astype(BF16)
        sg = gw * mixing
        sg_low = sg.astype(BF16)
        attl_ref[h] = dot(weights, v, NN)
        vloc[h] = dot(weights, g, TN)
        qloc[h] = dot(sg_low, k, NN)
        kloc[h] = dot(sg_low, q, TN)
        flow_ref[h : h + 1, :] = jnp.sum(sg * scores, 0, keepdims=True)
        plain = gw * scores * decay
        near = jnp.zeros((ROWS, 1), F32)
        for l in range(3):
            hit = (split == l) if l < 2 else (split >= 2)
            part = jnp.sum(jnp.where(hit, plain, 0.0), 1, keepdims=True)
            zc_ref[:, h * 8 + l : h * 8 + l + 1] = part
            near = near + gate[l] * part
        zc_ref[:, 16 + h : 17 + h] = near

    zc_ref[...] = jnp.zeros_like(zc_ref)
    flow_ref[...] = jnp.zeros_like(flow_ref)
    gather_step(1)
    attend(0)
    gather_step(2)
    for h in range(2):
        arrived(qc.at[h], Q_STEP + h, at_y(-1))
        send(qc.at[h], qc2.at[h], Q_STEP + 6 + h, at_y(-1))
        arrived(qb.at[h], Q_STEP + 2 + h, at_y(1))
        send(qb.at[h], qb2.at[h], Q_STEP + 8 + h, at_y(1))
    attend(1)
    gather_step(3)

    for j in range(1, NY):
        arrived(dcol.at[yy(-j)], D_COL + j, at_y(j))
    row1, row2 = dcol[1, 0:8, :], dcol[2, 0:8, :]
    w2, w3 = jnp.exp(dcol[2, 8:16, :]), jnp.exp(dcol[3, 8:16, :])
    wnext = jnp.exp(dcol[yy(1), 8:16, :])
    ca = jnp.where(lax.rem(y, 2) == 0, wnext, zero)
    cb = jnp.where(y == 0, w3 * jnp.exp(row1 + row2), zero)
    cb2 = jnp.where(y == 1, w3 * jnp.exp(row2), zero)
    cc = jnp.where(y == 1, w2, zero)
    cc2 = jnp.where(y == 0, w2 * jnp.exp(row1), zero)
    for h in range(2):
        arrived(qa.at[h], Q_STEP + 4 + h, at_y(-1))
        arrived(qc2.at[h], Q_STEP + 6 + h, at_y(-1))
        arrived(qb2.at[h], Q_STEP + 8 + h, at_y(1))
        s = slice(h, h + 1)
        pbuf[h] = (
            ca[s] * qa[h] + cb[s] * qb[h] + cb2[s] * qb2[h] + cc[s] * qc[h] + cc2[s] * qc2[h]
        )

    def contribution(h, target):
        e = etab[target, h : h + 1, :]
        c = ctab[target, h : h + 1, :]
        none = jnp.zeros_like(c)
        far = lax.div(target, 4) != lax.div(z, 4)
        same = lax.div(target, 2) == lax.div(z, 2)
        c3 = jnp.where(far, c, none)
        c1 = jnp.where(same, c, none)
        c2 = c - c3 - c1
        return e * pbuf[h] + c1 * qs_ref[h, 0] + c2 * qs_ref[h, 1] + c3 * qs_ref[h, 2]

    def reduce_step(k):
        for h in range(2):
            for up in (0, 1):
                first = 0 if h == 1 - up else 1
                if k < first:
                    continue
                sign = 1 if up else -1
                base = R_UP if up else R_DOWN
                mine_part = contribution(h, zz(sign * (4 - k)))
                if k > first:
                    arrived(rrecv.at[up, h, k - 1], base + 2 * (k - 1) + h, at_z(sign))
                    mine_part = mine_part + rrecv[up, h, k - 1]
                rsend[up, h, k] = mine_part
                send(rsend.at[up, h, k], rrecv.at[up, h, k], base + 2 * k + h, at_z(sign))

    reduce_step(0)

    for h in range(2):
        for k in range(1, 5):
            if k == 4:
                if h == 0:
                    arrived(sbuf.at[zz(-4), h], S_UP + 6 + h, at_z(1))
                else:
                    arrived(sbuf.at[zz(4), h], S_DOWN + 6 + h, at_z(-1))
                continue
            if k == 3:
                if h == 1:
                    arrived(sbuf.at[zz(-3), h], S_UP + 4 + h, at_z(1))
                else:
                    arrived(sbuf.at[zz(3), h], S_DOWN + 4 + h, at_z(-1))
        lev = [jnp.zeros((DH, DH), F32) for _ in range(3)]
        whole = jnp.zeros((DH, DH), F32)
        for i in range(NZ):
            s = sbuf[i, h]
            c = ctab[i, h : h + 1, :]
            none = jnp.zeros_like(c)
            far = lax.div(z, 4) != i // 4
            same = lax.div(z, 2) == i // 2
            c3 = jnp.where(far, c, none)
            c1 = jnp.where(same, c, none)
            c2 = c - c3 - c1
            lev[0] = lev[0] + c1 * s
            lev[1] = lev[1] + c2 * s
            lev[2] = lev[2] + c3 * s
            whole = whole + etab[i, h : h + 1, :] * s
        for m in range(3):
            lev_ref[h, :, m * DH : (m + 1) * DH] = lev[m].astype(BF16)
        tbuf[pl.ds(y, 1), h] = whole[None]
        send(tbuf.at[y, h], tbuf.at[y, h], T_UP + h, at_y(1))
        send(tbuf.at[y, h], tbuf.at[y, h], T_DOWN + h, at_y(-1))

    reduce_step(1)
    arrived(tbuf.at[yy(-1), 0], T_UP + 0, at_y(1))
    send(tbuf.at[yy(-1), 0], tbuf.at[yy(-1), 0], T_UP + 2, at_y(1))
    arrived(tbuf.at[yy(1), 1], T_DOWN + 1, at_y(-1))
    send(tbuf.at[yy(1), 1], tbuf.at[yy(1), 1], T_DOWN + 2, at_y(-1))
    arrived(tbuf.at[yy(-1), 1], T_UP + 1, at_y(1))
    arrived(tbuf.at[yy(1), 0], T_DOWN + 0, at_y(-1))
    reduce_step(2)
    arrived(tbuf.at[yy(-2), 0], T_UP + 2, at_y(1))
    arrived(tbuf.at[yy(2), 1], T_DOWN + 2, at_y(-1))

    f4 = jnp.where(lax.rem(y, 2) == 1, jnp.exp(mine), zero)
    f5 = jnp.where(y >= 2, jnp.exp(mine + jnp.where(y == 3, row2, zero)), zero)
    f5low = f5 * jnp.exp(row1)

    def far_rows(h):
        s = slice(h, h + 1)
        lev_ref[h, :, 3 * DH : 4 * DH] = (f4[s] * tbuf[yy(-1), h]).astype(BF16)
        lev_ref[h, :, 4 * DH : 5 * DH] = (f5[s] * tbuf[1, h] + f5low[s] * tbuf[0, h]).astype(BF16)
        projected = dot(q_ref[:, cols(h)], lev_ref[h], NN)
        g = g_ref[:, cols(h)].astype(F32)
        attended = attl_ref[h]
        extra = zc_ref[:, 16 + h : 17 + h]
        ecum = jnp.exp(cum_col(h))
        for m in range(FAR):
            part = projected[:, m * DH : (m + 1) * DH]
            coef = lift(h, m)
            attended = attended + coef * part
            inner = jnp.sum(part * g, 1, keepdims=True)
            zc_ref[:, h * 8 + 3 + m : h * 8 + 4 + m] = ecum * inner
            extra = extra + coef * inner
        zc_ref[:, 16 + h : 17 + h] = extra
        att_ref[:, cols(h)] = attended.astype(BF16)

    for h in range(2):
        far_rows(h)

    r, j = iota((512, ROWS), 0), iota((512, ROWS), 1)
    wanted = (r & 1) * DH + jnp.right_shift(r, 3) * 2 + (jnp.right_shift(r, 1) & 1)
    half = jnp.right_shift(r, 2) & 1
    match = wanted == j
    first_half = jnp.where(match & (half == 0), 1.0, 0.0).astype(BF16)
    second_half = jnp.where(match & (half == 1), 1.0, 0.0).astype(BF16)
    att = att_ref[...]
    lhs0 = dot(first_half, att, NT).astype(BF16)
    lhs1 = dot(second_half, att, NT).astype(BF16)
    wbuf[...] = dot(lhs0, cot_ref[:, 0:512], NN) + dot(lhs1, cot_ref[:, 512:1024], NN)
    theirs = pl.multiple_of((1 - dp) * 256, 256)
    ours = pl.multiple_of(dp * 256, 256)
    send(wbuf.at[pl.ds(theirs, 256)], wdp, W_DP, other)

    reduce_step(3)
    for h in range(2):
        qfar = dot(lifted_ref[h], lev_ref[h], NT)
        qg_ref[:, cols(h)] = (qloc[h] + qfar).astype(BF16)

    arrived(wdp, W_DP, other)
    usum[...] = wbuf[pl.ds(ours, 256), :] + wdp[...]

    def chunk(jy, start):
        return pl.ds(pl.multiple_of(yy(jy) * 64 + start, 32), 32)

    send(usum.at[chunk(2, 0)], wa1, W_Y + 0, at_y(1))
    send(usum.at[chunk(-2, 32)], wb1, W_Y + 1, at_y(-1))
    send(usum.at[chunk(1, 32)], wa2.at[pl.ds(32, 32)], W_Y + 2, at_y(1))
    send(usum.at[chunk(-1, 0)], wb2.at[pl.ds(0, 32)], W_Y + 3, at_y(-1))

    zt_ref[...] = jnp.transpose(zc_ref[...])
    gg_ref[...] = zt_ref[0:16, :]
    for h in range(2):
        arrived(rrecv.at[1, h, 3], R_UP + 6 + h, at_z(1))
        arrived(rrecv.at[0, h, 3], R_DOWN + 6 + h, at_z(-1))
        e = etab[z, h : h + 1, :]
        returned = (e * pbuf[h] + rrecv[1, h, 3] + rrecv[0, h, 3]).astype(BF16)
        k, v = k_ref[:, cols(h)], v_ref[:, cols(h)]
        w = to_end(h)
        kfar = w * dot(v, returned, NT)
        vfar = w * dot(k, returned, NN)
        kg_ref[:, cols(h)] = (kloc[h] + kfar).astype(BF16)
        vg_ref[:, cols(h)] = (vloc[h] + vfar).astype(BF16)
        zc_ref[:, 24 + h : 25 + h] = jnp.sum(k.astype(F32) * kfar, 1, keepdims=True)

    arrived(wa1, W_Y + 0, at_y(1))
    sa2[...] = usum[chunk(1, 0), :] + wa1[...]
    send(sa2, wa2.at[pl.ds(0, 32)], W_Y + 4, at_y(1))
    arrived(wb1, W_Y + 1, at_y(-1))
    sb2[...] = usum[chunk(-1, 32), :] + wb1[...]
    send(sb2, wb2.at[pl.ds(32, 32)], W_Y + 5, at_y(-1))

    back = jnp.transpose(zc_ref[...])
    flow = zt_ref[16:24, :] - flow_ref[...] - back[24:32, :]
    block_flow = jnp.broadcast_to(jnp.sum(flow, 1, keepdims=True), (8, 128))
    fbuf[pl.ds(z, 1)] = block_flow[None]
    for jz in range(1, NZ):
        send(fbuf.at[z], fbuf.at[z], F_ROW + jz, at_z(jz))
    onward = (iota((ROWS, ROWS), 0) >= iota((ROWS, ROWS), 1)).astype(BF16)
    within = exact_dot(flow, onward)

    arrived(wa2.at[pl.ds(32, 32)], W_Y + 2, at_y(1))
    arrived(wb2.at[pl.ds(0, 32)], W_Y + 3, at_y(-1))
    arrived(wa2.at[pl.ds(0, 32)], W_Y + 4, at_y(1))
    arrived(wb2.at[pl.ds(32, 32)], W_Y + 5, at_y(-1))
    own = pl.ds(pl.multiple_of(y * 64, 64), 64)
    zsum[...] = usum[own, :] + wa2[...] + wb2[...]

    def part_of(jz):
        return pl.ds(pl.multiple_of(zz(jz) * 8, 8), 8)

    for jz in range(1, NZ):
        send(zsum.at[part_of(jz)], wz.at[jz], W_Z + jz, at_z(jz))

    tail = zero
    row_flow = zero
    for jz in range(1, NZ):
        arrived(fbuf.at[zz(-jz)], F_ROW + jz, at_z(jz))
    for i in range(NZ):
        f = fbuf[i]
        row_flow = row_flow + f
        tail = tail + jnp.where(i > z, f, zero)
    fcol[pl.ds(y, 1)] = row_flow[None]
    for jy in range(1, NY):
        send(fcol.at[y], fcol.at[y], F_COL + jy, at_y(jy))

    result = zsum[part_of(0), :]
    for jz in range(1, NZ):
        arrived(wz.at[jz], W_Z + jz, at_z(jz))
        result = result + wz[jz]
    wg_ref[:, 0:512] = result[0:4, :]
    wg_ref[:, 512:1024] = result[4:8, :]

    for jy in range(1, NY):
        arrived(fcol.at[yy(-jy)], F_COL + jy, at_y(jy))
    for i in range(NY):
        tail = tail + jnp.where(i > y, fcol[i], zero)
    dg_ref[...] = (within + tail[:, 0:1])[0:2, :]

    for c in sent:
        c.wait_send()


def local(queries, key_vectors, value_vectors, out_cotangent, out_weight, log_decay, level_gates):
    v32 = lambda *s: pltpu.VMEM(s, F32)
    v16 = lambda *s: pltpu.VMEM(s, BF16)
    vmem = pl.BlockSpec(memory_space=pltpu.VMEM)
    scratch = [
        v32(128, ROWS), v32(ROWS, 128), v32(ROWS, 128), v32(128, ROWS), v32(8, ROWS),
        v32(NZ, 8, 128), v32(NY, 16, 128), v32(NZ, 8, 128), v32(NY, 8, 128),
        v32(NZ, 8, 128), v32(NZ, 8, 128),
        v32(NZ, 2, DH, DH), v32(NY, 2, DH, DH), v32(2, FAR, DH, DH),
        v32(2, DH, DH), v32(2, DH, DH), v32(2, DH, DH), v32(2, DH, DH), v32(2, DH, DH),
        v32(2, DH, DH), v32(2, 2, 4, DH, DH), v32(2, 2, 4, DH, DH),
        v16(ROWS, 256), v16(2, ROWS, FAR * DH), v16(2, DH, FAR * DH), v32(2, ROWS, DH),
        v32(2, ROWS, DH), v32(2, ROWS, DH), v32(2, ROWS, DH), v16(ROWS, 256),
        v32(512, 512), v32(256, 512), v32(256, 512), v32(32, 512), v32(32, 512),
        v32(64, 512), v32(64, 512), v32(32, 512), v32(32, 512), v32(64, 512), v32(NZ, 8, 512),
        pltpu.SemaphoreType.DMA((COPIES,)), pltpu.SemaphoreType.DMA((COPIES,)),
    ]
    outs = pl.pallas_call(
        kernel,
        out_shape=(
            jax.ShapeDtypeStruct((ROWS, 256), BF16),
            jax.ShapeDtypeStruct((ROWS, 256), BF16),
            jax.ShapeDtypeStruct((ROWS, 256), BF16),
            jax.ShapeDtypeStruct((2, ROWS), F32),
            jax.ShapeDtypeStruct((16, ROWS), F32),
            jax.ShapeDtypeStruct((4, 1024), F32),
        ),
        in_specs=[vmem] * 7,
        out_specs=(vmem,) * 6,
        scratch_shapes=scratch,
        compiler_params=pltpu.CompilerParams(collective_id=0, has_side_effects=True),
    )(
        queries[0], key_vectors[0], value_vectors[0], out_cotangent[0],
        out_weight.reshape(256, 1024), log_decay[0], level_gates[0].reshape(16, ROWS),
    )
    qg, kg, vg, dg, gg, wg = outs
    return (
        qg[None], kg[None], vg[None], dg[None],
        gg.reshape(1, 2, 8, ROWS), wg.reshape(2, 2, 1024),
    )


def solution(mesh):
    placed = (
        P("dp", "ctx", "head"),
        P("dp", "ctx", "head"),
        P("dp", "ctx", "head"),
        P("dp", "ctx", None),
        P(None, "head", None),
        P("dp", "head", "ctx"),
        P("dp", "head", None, "ctx"),
    )
    return jax.shard_map(
        local,
        mesh=mesh,
        in_specs=placed,
        out_specs=(
            P("dp", "ctx", "head"),
            P("dp", "ctx", "head"),
            P("dp", "ctx", "head"),
            P("dp", "head", "ctx"),
            P("dp", "head", None, "ctx"),
            P(("dp", "ctx"), "head", None),
        ),
        check_vma=False,
    )
```

time: 623 us -> 63.2 us (0.10); the launches traced: 612 us -> 62.9 us
  waiting for transfers between devices: 406 us -> 0 us
  blocking collectives: 129 us -> 0 us
  Pallas kernels: 0 us -> 54.5 us
  matrix products: 28.9 us -> 0 us
  local copies, waits for them, and re-layouts: 23.1 us -> 7.78 us
  between operations: 15.4 us -> 0.66 us
  other arithmetic: 8.72 us -> 0 us
    reduce_scatter x1 -> x0, waiting for transfers between devices: 220 us -> none  [local(): lax.psum_scatter(jnp.einsum('nmh,mhab->nhab', coef_part, level_major, pre...]
    unnamed x4 -> x0, waiting for transfers between devices: 173 us -> none
    unnamed x2 -> x0, blocking collectives: 129 us -> none
    pallas_call x0 -> x1, Pallas kernels: none -> 54.5 us  [local(): pl.pallas_call(kernel, out_shape=(jax.ShapeDtypeStruct((ROWS, 256), BF16)...]
    dot_general x28 -> x0, matrix products: 28.9 us -> none  [the longest x1 6.41 us: local(): jnp.einsum('nmh,nhab->mhab', coef_part, lax.all_gather(states[None], 'ctx...]
    all_gather x1 -> x0, waiting for transfers between devices: 12.6 us -> none  [local(): lax.all_gather(states[None], 'ctx', axis=0, tiled=True)]
  transfers between devices with their start and end apart: 3 -> 0, of which waited for: 3 -> 0; matrix products, arithmetic and copies ran while one was open for 3% -> 0% of each run, Pallas kernels for 0% -> 0%
where the time goes in v1:
time: 63.2 us; the launch traced here: 62.9 us
  Pallas kernels  54.5 us (86%)
  local copies, waits for them, and re-layouts  7.78 us (12%)
  between operations  0.66 us (1%)
    pallas_call x1, Pallas kernels, local(): pl.pallas_call(kernel, out_shape=(jax.ShapeDtypeStruct((ROWS, 256), BF16)...  54.5 us
    unnamed x15, local copies, waits for them, and re-layouts  5.12 us
    reshape x1, local copies, waits for them, and re-layouts, local(): out_weight.reshape(256, 1024)  2.03 us

profile of v1, /device:TPU:14, one launch (start us, length us, event | category | flops | bytes accessed | tf_op | source)
XLA Modules:
  0.0 62.9 jit_solution(5120813077597769678)
XLA Ops:
  0.6 2.0 %reshape.21.ow_ref = bf16[256,1024]{1,0:T(8,128)(2,1)} reshape(bf16[128,2,1024]{2,1,0:T(2,128)(2,1)} %param.11) | data formatting | bytes 1048576 | tf_op jit(solution)/shard_map/reshape | solution.py:487
  2.7 54.5 %shard_map.118 = (bf16[256,256]{1,0:T(8,128)(2,1)}, bf16[256,256]{1,0:T(8,128)(2,1)}, bf16[256,256]{1,0:T(8,128)(2,1)}, f32[2,256]{1,0:T(2,128)}, f32[16,256]{1,0:T(8,128)}, /*index=5*/f32[4,1024]{1,0:T(4,128)}) custom-call(bf16[256,256]{1,0:T(8,128)(2,1)} %bitcast.12, bf16[256,256]{1,0:T(8,128)(2,1)} %bitcast.13, bf16[256,256]{1,0:T(8,128)(2,1)} %bitcast.14, ...), custom_call_target="tpu_custom_call" | custom-call | tf_op jit(solution)/shard_map/pallas_call | solution.py:471
  57.2 0.0 copy-start.3
  57.2 0.7 %copy-done.3 = f32[4,1024]{1,0:T(4,128)S(1)} copy-done((f32[4,1024]{1,0:T(4,128)S(1)}, f32[4,1024]{1,0:T(4,128)}, u32[]{:S(2)}) %copy-start.3) | copy-done | bytes 16408
  57.9 0.6 reshape.23
  58.5 0.0 copy-start.1
  58.5 1.6 %copy.18 = bf16[1,256,256]{2,1,0:T(8,128)(2,1)} copy(bf16[1,256,256]{2,1,0:T(8,128)(2,1)} %bitcast.17) | data formatting | bytes 262144
  60.1 0.0 copy-done.1
  60.1 0.0 copy-start
  60.1 0.7 %copy.19 = bf16[1,256,256]{2,1,0:T(8,128)(2,1)} copy(bf16[1,256,256]{2,1,0:T(8,128)(2,1)S(1)} %bitcast.16) | data formatting | bytes 262144
  60.8 0.3 copy-done
  61.1 0.0 copy-start.4
  61.1 0.0 copy-start.2
  61.1 0.7 %copy.20 = bf16[1,256,256]{2,1,0:T(8,128)(2,1)} copy(bf16[1,256,256]{2,1,0:T(8,128)(2,1)S(1)} %bitcast.15) | data formatting | bytes 262144
  61.7 0.0 copy-done.4
  61.8 0.6 copy.21
  62.3 0.0 copy-done.2
  62.3 0.6 copy.22
Async XLA Ops:
  57.2 0.7 %copy-start.3 = (f32[4,1024]{1,0:T(4,128)S(1)}, f32[4,1024]{1,0:T(4,128)}, u32[]{:S(2)}) copy-start(f32[4,1024]{1,0:T(4,128)} %get-tuple-element.17) | copy-start | bytes 49156
  58.5 1.6 %copy-start.1 = (bf16[256,256]{1,0:T(8,128)(2,1)S(1)}, bf16[256,256]{1,0:T(8,128)(2,1)}, u32[]{:S(2)}) copy-start(bf16[256,256]{1,0:T(8,128)(2,1)} %get-tuple-element.13) | copy-start | bytes 393220
  60.1 1.0 %copy-start = (bf16[256,256]{1,0:T(8,128)(2,1)S(1)}, bf16[256,256]{1,0:T(8,128)(2,1)}, u32[]{:S(2)}) copy-start(bf16[256,256]{1,0:T(8,128)(2,1)} %get-tuple-element.14) | copy-start | bytes 393220
  61.1 0.7 %copy-start.4 = (f32[2,256]{1,0:T(2,128)S(1)}, f32[2,256]{1,0:T(2,128)}, u32[]{:S(2)}) copy-start(f32[2,256]{1,0:T(2,128)} %get-tuple-element.15) | copy-start | bytes 6148
  61.1 1.3 %copy-start.2 = (f32[16,256]{1,0:T(8,128)S(1)}, f32[16,256]{1,0:T(8,128)}, u32[]{:S(2)}) copy-start(f32[16,256]{1,0:T(8,128)} %get-tuple-element.16) | copy-start | bytes 49156

commit v2 on v1

--- a/solution.py
+++ b/solution.py
@@ -138,7 +138,7 @@
         send(sbuf.at[z, h], sbuf.at[z, h], S_UP + h, at_z(1))
         send(sbuf.at[z, h], sbuf.at[z, h], S_DOWN + h, at_z(-1))
 
-    mixed = dot(cot_ref[...], ow_ref[...], NT).astype(BF16)
+    mixed = dot(cot_ref[...], ow_ref[...].reshape(256, 1024), NT).astype(BF16)
     ri, ci = iota((ROWS, ROWS), 0), iota((ROWS, ROWS), 1)
     perm = (ri == 2 * (ci & (DH - 1)) + jnp.right_shift(ci, 7)).astype(BF16)
     g_ref[...] = dot(mixed, perm, NN).astype(BF16)
@@ -438,8 +438,9 @@
     for jz in range(1, NZ):
         arrived(wz.at[jz], W_Z + jz, at_z(jz))
         result = result + wz[jz]
-    wg_ref[:, 0:512] = result[0:4, :]
-    wg_ref[:, 512:1024] = result[4:8, :]
+    for i in range(2):
+        wg_ref[i, :, 0:512] = result[2 * i : 2 * i + 2, :]
+        wg_ref[i, :, 512:1024] = result[4 + 2 * i : 6 + 2 * i, :]
 
     for jy in range(1, NY):
         arrived(fcol.at[yy(-jy)], F_COL + jy, at_y(jy))
@@ -449,6 +450,11 @@
 
     for c in sent:
         c.wait_send()
+
+
+def hand_over(*refs):
+    for i in range(6):
+        refs[6 + i][...] = refs[i][...]
 
 
 def local(queries, key_vectors, value_vectors, out_cotangent, out_weight, log_decay, level_gates):
@@ -476,7 +482,7 @@
             jax.ShapeDtypeStruct((ROWS, 256), BF16),
             jax.ShapeDtypeStruct((2, ROWS), F32),
             jax.ShapeDtypeStruct((16, ROWS), F32),
-            jax.ShapeDtypeStruct((4, 1024), F32),
+            jax.ShapeDtypeStruct((2, 2, 1024), F32),
         ),
         in_specs=[vmem] * 7,
         out_specs=(vmem,) * 6,
@@ -484,12 +490,17 @@
         compiler_params=pltpu.CompilerParams(collective_id=0, has_side_effects=True),
     )(
         queries[0], key_vectors[0], value_vectors[0], out_cotangent[0],
-        out_weight.reshape(256, 1024), log_decay[0], level_gates[0].reshape(16, ROWS),
+        out_weight, log_decay[0], level_gates[0].reshape(16, ROWS),
     )
-    qg, kg, vg, dg, gg, wg = outs
+    qg, kg, vg, dg, gg, wg = pl.pallas_call(
+        hand_over,
+        out_shape=tuple(jax.ShapeDtypeStruct(o.shape, o.dtype) for o in outs),
+        in_specs=[vmem] * 6,
+        out_specs=(vmem,) * 6,
+    )(*outs)
     return (
         qg[None], kg[None], vg[None], dg[None],
-        gg.reshape(1, 2, 8, ROWS), wg.reshape(2, 2, 1024),
+        gg.reshape(1, 2, 8, ROWS), wg,
     )
 
 

time: 63.2 us -> 57.2 us (0.905)
  local copies, waits for them, and re-layouts: 7.78 us -> 0 us
  Pallas kernels: 54.5 us -> 56.4 us
    unnamed x15 -> x0, local copies, waits for them, and re-layouts: 5.12 us -> none
    reshape x2 -> x0, local copies, waits for them, and re-layouts: 2.65 us -> none  [the longest x1 2.03 us: local(): out_weight.reshape(256, 1024)]
    pallas_call x0 -> x1, Pallas kernels: none -> 1.8 us  [local(): pl.pallas_call(hand_over, out_shape=tuple((jax.ShapeDtypeStruct(o.shape,...]
where the time goes in v2:
time: 57.2 us; the launch traced here: 57.1 us
  Pallas kernels  56.4 us (99%)
  between operations  0.64 us (1%)
    pallas_call x1, Pallas kernels, local(): pl.pallas_call(kernel, out_shape=(jax.ShapeDtypeStruct((ROWS, 256), BF16)...  54.6 us
    pallas_call x1, Pallas kernels, local(): pl.pallas_call(hand_over, out_shape=tuple((jax.ShapeDtypeStruct(o.shape,...  1.8 us

profile of v2, /device:TPU:14, one launch (start us, length us, event | category | flops | bytes accessed | tf_op | source)
XLA Modules:
  0.0 57.1 jit_solution(7173760033763786614)
XLA Ops:
  0.6 54.6 %shard_map.118 = (bf16[256,256]{1,0:T(8,128)(2,1)}, bf16[256,256]{1,0:T(8,128)(2,1)}, bf16[256,256]{1,0:T(8,128)(2,1)}, f32[2,256]{1,0:T(2,128)}, f32[16,256]{1,0:T(8,128)}, /*index=5*/f32[2,2,1024]{2,1,0:T(2,128)}) custom-call(bf16[256,256]{1,0:T(8,128)(2,1)} %bitcast.12, bf16[256,256]{1,0:T(8,128)(2,1)} %bitcast.13, bf16[256,256]{1,0:T(8,128)(2,1)} %bitcast.14, ...), custom_call_target="tpu_custom_call" | custom-call | tf_op jit(solution)/shard_map/pallas_call | solution.py:477
  55.3 1.8 %shard_map.119 = (bf16[256,256]{1,0:T(8,128)(2,1)}, bf16[256,256]{1,0:T(8,128)(2,1)}, bf16[256,256]{1,0:T(8,128)(2,1)}, f32[2,256]{1,0:T(2,128)}, f32[16,256]{1,0:T(8,128)}, /*index=5*/f32[2,2,1024]{2,1,0:T(2,128)}) custom-call(bf16[256,256]{1,0:T(8,128)(2,1)} %get-tuple-element.18.refs_0_, bf16[256,256]{1,0:T(8,128)(2,1)} %get-tuple-element.19.refs_1_, ...), custom_call_target="tpu_custom_call" | custom-call | tf_op jit(solution)/shard_map/pallas_call | solution.py:495

commit v3 on v2

--- a/solution.py
+++ b/solution.py
@@ -419,7 +419,7 @@
     def part_of(jz):
         return pl.ds(pl.multiple_of(zz(jz) * 8, 8), 8)
 
-    for jz in range(1, NZ):
+    for jz in (4, 3, 5, 2, 6, 1, 7):
         send(zsum.at[part_of(jz)], wz.at[jz], W_Z + jz, at_z(jz))
 
     tail = zero

time: 57.2 us -> 56.9 us (level)
  Pallas kernels: 56.4 us -> 55.8 us
    pallas_call x1, Pallas kernels: 54.6 us -> 54 us  [local(): pl.pallas_call(kernel, out_shape=(jax.ShapeDtypeStruct((ROWS, 256), BF16)...]
where the time goes in v3:
time: 56.9 us; the launch traced here: 56.5 us
  Pallas kernels  55.8 us (98%)
  between operations  0.64 us (1%)
    pallas_call x1, Pallas kernels, local(): pl.pallas_call(kernel, out_shape=(jax.ShapeDtypeStruct((ROWS, 256), BF16)...  54 us
    pallas_call x1, Pallas kernels, local(): pl.pallas_call(hand_over, out_shape=tuple((jax.ShapeDtypeStruct(o.shape,...  1.8 us

profile of v3, /device:TPU:14, one launch (start us, length us, event | category | flops | bytes accessed | tf_op | source)
XLA Modules:
  0.0 56.5 jit_solution(8637398884720894989)
XLA Ops:
  0.6 54.0 %shard_map.118 = (bf16[256,256]{1,0:T(8,128)(2,1)}, bf16[256,256]{1,0:T(8,128)(2,1)}, bf16[256,256]{1,0:T(8,128)(2,1)}, f32[2,256]{1,0:T(2,128)}, f32[16,256]{1,0:T(8,128)}, /*index=5*/f32[2,2,1024]{2,1,0:T(2,128)}) custom-call(bf16[256,256]{1,0:T(8,128)(2,1)} %bitcast.12, bf16[256,256]{1,0:T(8,128)(2,1)} %bitcast.13, bf16[256,256]{1,0:T(8,128)(2,1)} %bitcast.14, ...), custom_call_target="tpu_custom_call" | custom-call | tf_op jit(solution)/shard_map/pallas_call | solution.py:477
  54.7 1.8 %shard_map.119 = (bf16[256,256]{1,0:T(8,128)(2,1)}, bf16[256,256]{1,0:T(8,128)(2,1)}, bf16[256,256]{1,0:T(8,128)(2,1)}, f32[2,256]{1,0:T(2,128)}, f32[16,256]{1,0:T(8,128)}, /*index=5*/f32[2,2,1024]{2,1,0:T(2,128)}) custom-call(bf16[256,256]{1,0:T(8,128)(2,1)} %get-tuple-element.18.refs_0_, bf16[256,256]{1,0:T(8,128)(2,1)} %get-tuple-element.19.refs_1_, ...), custom_call_target="tpu_custom_call" | custom-call | tf_op jit(solution)/shard_map/pallas_call | solution.py:495

commit v4 on v3

--- a/solution.py
+++ b/solution.py
@@ -276,6 +276,8 @@
                 send(rsend.at[up, h, k], rrecv.at[up, h, k], base + 2 * k + h, at_z(sign))
 
     reduce_step(0)
+
+    reduce_step(1)
 
     for h in range(2):
         for k in range(1, 5):
@@ -311,14 +313,14 @@
         send(tbuf.at[y, h], tbuf.at[y, h], T_UP + h, at_y(1))
         send(tbuf.at[y, h], tbuf.at[y, h], T_DOWN + h, at_y(-1))
 
-    reduce_step(1)
+    reduce_step(2)
     arrived(tbuf.at[yy(-1), 0], T_UP + 0, at_y(1))
     send(tbuf.at[yy(-1), 0], tbuf.at[yy(-1), 0], T_UP + 2, at_y(1))
     arrived(tbuf.at[yy(1), 1], T_DOWN + 1, at_y(-1))
     send(tbuf.at[yy(1), 1], tbuf.at[yy(1), 1], T_DOWN + 2, at_y(-1))
     arrived(tbuf.at[yy(-1), 1], T_UP + 1, at_y(1))
     arrived(tbuf.at[yy(1), 0], T_DOWN + 0, at_y(-1))
-    reduce_step(2)
+    reduce_step(3)
     arrived(tbuf.at[yy(-2), 0], T_UP + 2, at_y(1))
     arrived(tbuf.at[yy(2), 1], T_DOWN + 2, at_y(-1))
 
@@ -362,7 +364,6 @@
     ours = pl.multiple_of(dp * 256, 256)
     send(wbuf.at[pl.ds(theirs, 256)], wdp, W_DP, other)
 
-    reduce_step(3)
     for h in range(2):
         qfar = dot(lifted_ref[h], lev_ref[h], NT)
         qg_ref[:, cols(h)] = (qloc[h] + qfar).astype(BF16)

time: 56.9 us -> 59.9 us (1.053); the launches traced: 56.5 us -> 58.8 us
  Pallas kernels: 55.8 us -> 58.2 us
    pallas_call x1, Pallas kernels: 54 us -> 56.4 us  [local(): pl.pallas_call(kernel, out_shape=(jax.ShapeDtypeStruct((ROWS, 256), BF16)...]
where the time goes in v4:
time: 59.9 us; the launch traced here: 58.8 us
  Pallas kernels  58.2 us (97%)
  between operations  0.64 us (1%)
    pallas_call x1, Pallas kernels, local(): pl.pallas_call(kernel, out_shape=(jax.ShapeDtypeStruct((ROWS, 256), BF16)...  56.4 us
    pallas_call x1, Pallas kernels, local(): pl.pallas_call(hand_over, out_shape=tuple((jax.ShapeDtypeStruct(o.shape,...  1.8 us

profile of v4, /device:TPU:14, one launch (start us, length us, event | category | flops | bytes accessed | tf_op | source)
XLA Modules:
  0.0 58.8 jit_solution(204590643920773804)
XLA Ops:
  0.6 56.4 %shard_map.118 = (bf16[256,256]{1,0:T(8,128)(2,1)}, bf16[256,256]{1,0:T(8,128)(2,1)}, bf16[256,256]{1,0:T(8,128)(2,1)}, f32[2,256]{1,0:T(2,128)}, f32[16,256]{1,0:T(8,128)}, /*index=5*/f32[2,2,1024]{2,1,0:T(2,128)}) custom-call(bf16[256,256]{1,0:T(8,128)(2,1)} %bitcast.12, bf16[256,256]{1,0:T(8,128)(2,1)} %bitcast.13, bf16[256,256]{1,0:T(8,128)(2,1)} %bitcast.14, ...), custom_call_target="tpu_custom_call" | custom-call | tf_op jit(solution)/shard_map/pallas_call | solution.py:478
  57.0 1.8 %shard_map.119 = (bf16[256,256]{1,0:T(8,128)(2,1)}, bf16[256,256]{1,0:T(8,128)(2,1)}, bf16[256,256]{1,0:T(8,128)(2,1)}, f32[2,256]{1,0:T(2,128)}, f32[16,256]{1,0:T(8,128)}, /*index=5*/f32[2,2,1024]{2,1,0:T(2,128)}) custom-call(bf16[256,256]{1,0:T(8,128)(2,1)} %get-tuple-element.18.refs_0_, bf16[256,256]{1,0:T(8,128)(2,1)} %get-tuple-element.19.refs_1_, ...), custom_call_target="tpu_custom_call" | custom-call | tf_op jit(solution)/shard_map/pallas_call | solution.py:496
